TPU v7x, 256 devices: a whole 4x4x8 slice. The times are simulated.
256 devices in a mesh: band: 4 (over x), tile: 64 (over y, z, core).
Axes of the slice: x: 4, y: 4, z: 8, core: 2. Of those that a mesh axis runs over, the one named last changes fastest.
Arguments:
- granules: bfloat16 [1024, 16, 4096], P('tile', 'band'), may hold values from -6 to 6
- valid_rows: int32 [1024, 64], P('tile'), may hold values 0 or 1
- scene_order: int32 [1024], P('tile'), may hold values from 0 to 1023, each once
- intersections: int32 [1024, 4], P('tile'), may hold values from 0 to 63, all different within a row; in each aligned block of 16 rows (0 to 15, 16 to 31, ...) at most 2 rows name the same one
- row_resample: bfloat16 [1024, 4, 4096], P('tile'), may hold values from 0 to 1.4, as said below
- col_resample: bfloat16 [1024, 4, 4096], P('tile'), may hold values from 0 to 1.4, as said below
- w_in: bfloat16 [16, 256], replicated, may hold values from -1.5 to 1.5
- w_hidden: bfloat16 [2, 256, 256], replicated, may hold values from -0.375 to 0.375
- w_out: bfloat16 [256], replicated, may hold values from -1.5 to 1.5
Outputs:
- composite: float32 [16, 262144], P('band', 'tile')
Inputs may be any that keep to these rules, and one draw needn't show every extreme that they name: `intersections`: each scene names 4 different output tiles; the 16 scenes of one device name any one tile at most 2 times, a bound that some block reaches. `scene_order`: each order number appears once. `row_resample`: nonnegative resampling weights. `col_resample`: nonnegative resampling weights.
All inputs are finite; a program needn't handle non-finite values. No bound on the sum of `valid_rows` on one device may be relied on, other than what follows from the above.
Results may differ from a plain program's by a relative error of at most 0.0031.
Values may be sent and summed in bfloat16 or wider, within the bound.
No kernel may reach another device: no remote copies, remote signals or barrier semaphores. Data moves between devices by JAX's collectives and lax.ppermute only.
A program may use at most 128 MiB of HBM per device.

v0:
```python
import jax
import jax.numpy as jnp
from jax import lax
from jax.sharding import PartitionSpec as P

HUBER_ITERS = 4
SMOOTH = 2
prior_weight = 0.25
huber_delta = 0.5
edge_scale = 1.0
smooth_rate = 0.2


def extended_2(block, sides, width):
    for axis, dim in sides:
        count = lax.axis_size(axis)
        forward = [(i, i + 1) for i in range(count - 1)]
        backward = [(target, source) for source, target in forward]
        low = lax.ppermute(
            lax.slice_in_dim(block, block.shape[dim] - width, None, axis=dim), axis, forward
        )
        high = lax.ppermute(lax.slice_in_dim(block, 0, width, axis=dim), axis, backward)
        block = jnp.concatenate([low, block, high], axis=dim)
    return block


def scene_weights(pixels, valid_part, recency, w_in, w_hidden, w_out, side_cells):
    scenes, row_count = valid_part.shape
    valid_pix = jnp.broadcast_to(
        valid_part.astype(jnp.float32)[:, :, None], (scenes, row_count, side_cells)
    )
    valid_pix = valid_pix.reshape(scenes, row_count * side_cells)

    def one_scene(inputs):
        scene_pixels, scene_valid, scene_recency = inputs
        hidden = jax.nn.silu(
            jnp.einsum("cn,ch->nh", scene_pixels, w_in, preferred_element_type=jnp.float32)
        ).astype(jnp.bfloat16)
        for repeat in range(w_hidden.shape[0]):
            hidden = jax.nn.silu(
                jnp.dot(hidden, w_hidden[repeat], preferred_element_type=jnp.float32)
            ).astype(jnp.bfloat16)
        logits = jnp.dot(hidden, w_out, preferred_element_type=jnp.float32)
        return (jax.nn.sigmoid(-logits) * scene_valid * scene_recency).astype(jnp.bfloat16)

    return lax.map(one_scene, (pixels, valid_pix, recency))


def reproject(planes, rows_matrix, cols_matrix):
    half_done = jnp.einsum(
        "ncil,njl->ncij", planes, cols_matrix, preferred_element_type=jnp.float32
    ).astype(jnp.bfloat16)
    return jnp.einsum(
        "nij,ncjl->ncil", rows_matrix, half_done, preferred_element_type=jnp.float32
    ).astype(jnp.bfloat16)


def huber_merge(observed, weights):
    values = observed.astype(jnp.float32)
    plain = weights.astype(jnp.float32)[:, None, :]
    estimate = jnp.sum(plain * values, 0) / (jnp.sum(plain, 0) + prior_weight)
    for repeat in range(HUBER_ITERS):
        residual = values - estimate[None]
        huber_w = plain * huber_delta / jnp.maximum(jnp.abs(residual), huber_delta)
        estimate = jnp.sum(huber_w * values, 0) / (jnp.sum(huber_w, 0) + prior_weight)
    return estimate


def smooth_step(extended, first_col, total_cols):
    positions = first_col + jnp.arange(extended.shape[2] - 1)
    inside = ((positions >= 0) & (positions + 1 < total_cols)).astype(jnp.float32)
    across = extended[:, :, 1:] - extended[:, :, :-1]
    sideways = across / (1.0 + (across / edge_scale) ** 2) * inside
    centre = extended[:, :, 1:-1]
    upward_diff = centre[:, 1:, :] - centre[:, :-1, :]
    upward = upward_diff / (1.0 + (upward_diff / edge_scale) ** 2)
    zeros_row = jnp.zeros_like(upward[:, :1, :])
    vertical = jnp.concatenate([upward, zeros_row], 1) - jnp.concatenate([zeros_row, upward], 1)
    return centre + smooth_rate * (sideways[:, :, 1:] - sideways[:, :, :-1] + vertical)


def per_device(
    granules,
    valid_rows,
    scene_order,
    intersections,
    row_resample,
    col_resample,
    w_in,
    w_hidden,
    w_out,
):
    scenes, group_bands, pixel_count = granules.shape
    side_cells = valid_rows.shape[1]
    intersection_count = intersections.shape[1]
    tile_count = lax.axis_size("tile")
    band_count = lax.axis_size("band")
    recency = jnp.exp(1.4 * scene_order.astype(jnp.float32) / (scenes * tile_count) - 0.7)
    by_rows = lax.all_to_all(granules, "band", split_axis=2, concat_axis=1, tiled=True)
    row_count = side_cells // band_count
    valid_here = lax.dynamic_slice_in_dim(
        valid_rows, lax.axis_index("band") * row_count, row_count, 1
    )
    partial_weights = scene_weights(by_rows, valid_here, recency, w_in, w_hidden, w_out, side_cells)
    weights = lax.all_gather(partial_weights, "band", axis=1, tiled=True)
    plane_count = group_bands + 1
    planes = jnp.concatenate([granules, weights[:, None, :]], 1)
    entry_count = scenes * intersection_count
    capacity = (entry_count + tile_count - 1) // tile_count + 1
    buffer_rows = tile_count * capacity
    flat_dest = intersections.reshape(entry_count)
    onehot = (flat_dest[:, None] == jnp.arange(tile_count, dtype=jnp.int32)[None, :]).astype(
        jnp.int32
    )
    slot_rank = jnp.sum((jnp.cumsum(onehot, 0) - onehot) * onehot, 1)
    slot_index = flat_dest * capacity + slot_rank
    raw_planes = jnp.repeat(planes, intersection_count, axis=0)
    matrices = jnp.stack([row_resample, col_resample], 2).reshape(entry_count, 2, pixel_count)
    raw_out = (
        jnp.zeros((buffer_rows, plane_count, pixel_count), jnp.bfloat16)
        .at[slot_index]
        .set(raw_planes)
    )
    matrix_out = jnp.zeros((buffer_rows, 2, pixel_count), jnp.bfloat16).at[slot_index].set(matrices)
    raw_in, matrix_in = (
        lax.all_to_all(raw_out, "tile", split_axis=0, concat_axis=0, tiled=True),
        lax.all_to_all(matrix_out, "tile", split_axis=0, concat_axis=0, tiled=True),
    )
    matrix_in = matrix_in.reshape(buffer_rows, 2, side_cells, side_cells)
    incoming = reproject(
        raw_in.reshape(buffer_rows, plane_count, side_cells, side_cells),
        matrix_in[:, 0],
        matrix_in[:, 1],
    )
    incoming = incoming.reshape(buffer_rows, plane_count, pixel_count)
    estimate = huber_merge(incoming[:, :group_bands], incoming[:, group_bands])
    field = estimate.reshape(group_bands, side_cells, side_cells)
    first_col = lax.axis_index("tile") * side_cells
    total_cols = tile_count * side_cells
    for repeat in range(SMOOTH):
        extended = extended_2(field, (("tile", 2),), 1)
        field = smooth_step(extended, first_col - 1, total_cols)
    return field.reshape(group_bands, pixel_count)


def solution(mesh):
    return jax.shard_map(
        per_device,
        mesh=mesh,
        in_specs=(
            P("tile", "band", None),
            P("tile", None),
            P("tile"),
            P("tile", None),
            P("tile", None, None),
            P("tile", None, None),
            P(),
            P(),
            P(),
        ),
        out_specs=P("band", "tile"),
        check_vma=False,
    )
```

profile of v0, /device:TPU:8, one launch (start us, length us, event | category | flops | bytes accessed | tf_op | source)
XLA Modules:
  0.0 474.6 jit_solution(6735166915798410247)
XLA Ops:
  0.0 6.5 %copy.57 = bf16[16,4,4096]{0,1,2:T(4,128)(2,1)} copy(bf16[16,4,4096]{2,1,0:T(4,128)(2,1)} %param.11) | data formatting | bytes 1048576 | tf_op args[0]
  6.5 6.5 %reshape.136 = bf16[4,2,32768]{2,1,0:T(2,128)(2,1)} reshape(bf16[4096,4,16]{2,1,0:T(4,128)(2,1)} %bitcast.84) | data formatting | bytes 1048576
  13.0 4.3 all-to-all-start
  19.9 2.4 pad_maximum_fusion.1
  22.3 3.4 broadcast_in_dim.40
  25.8 8.2 %scatter_fusion.1 = bf16[128,2,4096]{2,1,0:T(2,128)(2,1)} fusion(bf16[128,2,4096]{2,1,0:T(2,128)(2,1)} %broadcast_in_dim.40, s32[64]{0:T(128)S(1)} %fusion.59, bf16[64,2,4096]{2,1,0:T(2,128)(2,1)S(1)} %pad_maximum_fusion.1), kind=kCustom, calls=%fused_computation.1 | custom fusion | bytes 3145984 | tf_op jit(solution)/shard_map/scatter | solution.py:124
  34.0 12.1 %all-to-all-start.2 = ((bf16[128,2,4096]{2,1,0:T(2,128)(2,1)}), bf16[128,2,4096]{2,1,0:T(2,128)(2,1)S(1)}, u32[]{:S(2)}, u32[]{:S(2)}) async-start(bf16[128,2,4096]{2,1,0:T(2,128)(2,1)} %scatter_fusion.1), calls=%async_computation.2 | async-start | bytes 4194304 | tf_op jit(solution)/shard_map/all_to_all | solution.py:127
  46.1 5.4 %reshape.137 = bf16[4096,4,16]{2,1,0:T(4,128)(2,1)} reshape(bf16[4,2,32768]{2,1,0:T(2,128)(2,1)} %all-to-all-done) | data formatting | bytes 1048576
  51.5 6.1 %copy.58 = bf16[16,4,4,1024]{3,2,1,0:T(4,128)(2,1)S(1)} copy(bf16[16,4,4,1024]{0,2,3,1:T(4,128)(2,1)} %bitcast.83) | data formatting | bytes 1048576 | tf_op jit(solution)/shard_map/all_to_all | solution.py:99
  57.8 74.0 %while.10 = (s32[]{:T(128)}, bf16[16,1024]{1,0:T(8,128)(2,1)S(1)}, bf16[16,16,1024]{2,1,0:T(8,128)(2,1)S(1)}, bf16[16,256]{1,0:T(8,128)(2,1)S(1)}, bf16[2,256,25...) while((s32[]{:T(128)}, bf16[16,1024]{1,0:T(8,128)(2,1)S(1)}, ...), condition=%wide.region_3.4_spmd, body=%wide.region_2.3_spmd.sunk | while | flops 281285632 | bytes 1384577 | solution.py:46
  59.3 1.6 fusion.80
  63.9 1.6 fusion.80
  68.6 1.6 fusion.80
  77.8 1.6 fusion.80
  82.4 1.6 fusion.80
  87.0 1.6 fusion.80
  91.7 1.6 fusion.80
  96.3 1.6 fusion.80
  100.9 1.6 fusion.80
  119.4 1.6 fusion.80
  124.0 1.6 fusion.80
  128.7 1.6 fusion.80
  131.7 12.8 %all_gather.3 = bf16[16,4096]{1,0:T(8,128)(2,1)S(1)} all-gather(bf16[16,1024]{1,0:T(8,128)(2,1)S(1)} %get-tuple-element.47), channel_id=1, replica_groups=mesh['band'=4,'tile'=64] {'band'}, dimensions={1}, use_global_device_ids=true | all-gather | bytes 163840 | tf_op jit(solution)/shard_map/all_gather | solution.py:105
  145.4 2.4 broadcast_in_dim.20.clone
  147.8 4.3 broadcast_in_dim.16
  152.1 11.9 %scatter_fusion = bf16[128,5,4096]{2,1,0:T(8,128)(2,1)} fusion(bf16[128,5,4096]{2,1,0:T(8,128)(2,1)} %broadcast_in_dim.16, s32[64]{0:T(128)S(1)} %fusion.59, bf16[64,5,4096]{2,1,0:T(8,128)(2,1)} %bitcast.82), kind=kCustom, calls=%fused_computation | custom fusion | bytes 7864576 | tf_op jit(solution)/shard_map/scatter | solution.py:122
  164.0 10.5 %all-to-all-start.1 = ((bf16[128,5,4096]{2,1,0:T(8,128)(2,1)}), bf16[128,5,4096]{2,1,0:T(8,128)(2,1)}, u32[]{:S(2)}, u32[]{:S(2)}) async-start(bf16[128,5,4096]{2,1,0:T(8,128)(2,1)} %scatter_fusion), calls=%async_computation.1 | async-start | bytes 16777216 | tf_op jit(solution)/shard_map/all_to_all | solution.py:126
  174.5 4.0 copy.65
  178.6 2.7 fusion.60
  181.3 3.9 copy.75
  185.2 3.8 copy.76
  189.0 169.8 %all-to-all-done.1 = bf16[128,5,4096]{2,1,0:T(8,128)(2,1)} async-done(((bf16[128,5,4096]{2,1,0:T(8,128)(2,1)}), bf16[128,5,4096]{2,1,0:T(8,128)(2,1)}, u32[]{:S(2)}, u32[]{:S(2)}) %all-to-all-start.1) | async-done | bytes 5242912 | tf_op jit(solution)/shard_map/all_to_all | solution.py:126
  358.8 10.6 %copy.62 = bf16[128,5,4096]{0,2,1:T(8,128)(2,1)} copy(bf16[128,5,4096]{2,1,0:T(8,128)(2,1)} %all-to-all-done.1) | data formatting | bytes 10485760 | tf_op jit(solution)/shard_map/all_to_all | solution.py:126
  369.5 15.7 %copy.67 = bf16[128,5,64,64]{3,2,1,0:T(8,128)(2,1)} copy(bf16[128,5,64,64]{0,3,2,1:T(8,128)(2,1)} %bitcast.81) | data formatting | bytes 10485760 | tf_op jit(solution)/shard_map/reshape | solution.py:131
  385.2 12.5 %convert_bitcast_fusion = bf16[128,5,64,64]{2,3,1,0:T(8,128)(2,1)} fusion(bf16[128,5,64,64]{3,2,1,0:T(8,128)(2,1)} %copy.67, bf16[128,1,64,64]{3,2,0,1:T(8,128)(2,1)} %copy.76, bf16[128,1,64,64]{3,2,0,1:T(8,128)(2,1)S(1)} %copy.75), kind=kOutput, calls=%fused_computation.29 | convolution fusion | flops 676331520 | bytes 12582912 | tf_op jit(solution)/shard_map/nij,ncjl->ncil/dot_general | solution.py:53
  397.7 18.1 %copy.70 = bf16[128,5,64,64]{0,3,2,1:T(8,128)(2,1)} copy(bf16[128,5,64,64]{2,3,1,0:T(8,128)(2,1)} %convert_bitcast_fusion) | data formatting | bytes 10485760 | tf_op jit(solution)/shard_map/convert_element_type | solution.py:55
  417.3 1.9 fusion.48
  419.3 2.3 fusion.23
  421.6 7.8 %fusion.47 = (f32[4,4096]{1,0:T(4,128)S(1)}, f32[4,4096]{1,0:T(4,128)S(1)}) fusion(f32[4,4096]{1,0:T(4,128)S(1)} %broadcast_divide_fusion, f32[128,4096]{0,1:T(8,128)S(1)} %get-tuple-element.72, bf16[128,5,4096]{0,2,1:T(8,128)(2,1)S(1)} %bitcast.77), kind=kLoop, calls=%fused_computation.53 | loop fusion | flops 16744448 | bytes 6488064 | tf_op jit(solution)/shard_map/reduce_sum | solution.py:65
  429.4 7.6 %fusion.46 = (f32[4,4096]{1,0:T(4,128)S(1)}, f32[4,4096]{1,0:T(4,128)S(1)}) fusion(f32[4,4096]{1,0:T(4,128)S(1)} %add_divide_fusion.5, f32[128,4096]{0,1:T(8,128)S(1)} %get-tuple-element.72, bf16[128,5,4096]{0,2,1:T(8,128)(2,1)S(1)} %bitcast.78), kind=kLoop, calls=%fused_computation.52 | loop fusion | flops 16744448 | bytes 6488064 | tf_op jit(solution)/shard_map/reduce_sum | solution.py:65
  437.1 7.6 %fusion.45 = (f32[4,4096]{1,0:T(4,128)S(1)}, f32[4,4096]{1,0:T(4,128)S(1)}) fusion(f32[4,4096]{1,0:T(4,128)S(1)} %add_divide_fusion.4, f32[128,4096]{0,1:T(8,128)S(1)} %get-tuple-element.72, bf16[128,5,4096]{0,2,1:T(8,128)(2,1)S(1)} %bitcast.79), kind=kLoop, calls=%fused_computation.51 | loop fusion | flops 16744448 | bytes 6488064 | tf_op jit(solution)/shard_map/reduce_sum | solution.py:65
  444.7 7.6 %fusion.44 = (f32[4,4096]{1,0:T(4,128)S(1)}, f32[4,4096]{1,0:T(4,128)S(1)}) fusion(f32[4,4096]{1,0:T(4,128)S(1)} %add_divide_fusion.3, f32[128,4096]{0,1:T(8,128)S(1)} %get-tuple-element.72, bf16[128,5,4096]{0,2,1:T(8,128)(2,1)S(1)} %bitcast.80), kind=kLoop, calls=%fused_computation.50 | loop fusion | flops 16744448 | bytes 6488064 | tf_op jit(solution)/shard_map/reduce_sum | solution.py:65
  452.6 1.9 collective-permute-start
  454.5 3.3 collective-permute-start.1
  457.8 5.1 %collective-permute-done.1 = f32[4,64,1]{2,1,0:T(8,128)S(1)} collective-permute-done((f32[4,64,1]{2,1,0:T(8,128)S(1)}, f32[4,64,1]{2,1,0:T(8,128)S(1)}, u32[]{:S(2)}, u32[]{:S(2)}) %collective-permute-start.1) | collective-permute-done | bytes 1056 | tf_op jit(solution)/shard_map/ppermute | solution.py:19
  463.3 1.9 collective-permute-start.2
  465.2 2.4 collective-permute-start.3
  467.7 5.9 %collective-permute-done.3 = f32[4,64,1]{2,1,0:T(8,128)S(1)} collective-permute-done((f32[4,64,1]{2,1,0:T(8,128)S(1)}, f32[4,64,1]{2,1,0:T(8,128)S(1)}, u32[]{:S(2)}, u32[]{:S(2)}) %collective-permute-start.3) | collective-permute-done | bytes 1056 | tf_op jit(solution)/shard_map/ppermute | solution.py:19
  (177 shorter events, 61.0 us)
Async XLA Ops:
  0.0 17.3 %copy-start.4 = (s32[16,4]{0,1:T(4,128)S(1)}, s32[16,4]{0,1:T(4,128)}, u32[]{:S(2)}) copy-start(s32[16,4]{0,1:T(4,128)} %param.14) | copy-start | bytes 772
  0.0 17.4 %copy-start.5 = (s32[16,64]{1,0:T(8,128)S(1)}, s32[16,64]{1,0:T(8,128)}, u32[]{:S(2)}) copy-start(s32[16,64]{1,0:T(8,128)} %param.12) | copy-start | bytes 12292
  0.0 18.3 %copy-start.2 = (bf16[16,4,4096]{2,1,0:T(4,128)(2,1)S(1)}, bf16[16,4,4096]{2,1,0:T(4,128)(2,1)}, u32[]{:S(2)}) copy-start(bf16[16,4,4096]{2,1,0:T(4,128)(2,1)} %param.15) | copy-start | bytes 1572868
  0.0 19.1 %copy-start.3 = (bf16[16,4,4096]{2,1,0:T(4,128)(2,1)S(1)}, bf16[16,4,4096]{2,1,0:T(4,128)(2,1)}, u32[]{:S(2)}) copy-start(bf16[16,4,4096]{2,1,0:T(4,128)(2,1)} %param.16) | copy-start | bytes 1572868
  6.5 27.5 %copy-start.8 = (s32[16]{0:T(128)S(1)}, s32[16]{0:T(128)}, u32[]{:S(2)}) copy-start(s32[16]{0:T(128)} %param.13) | copy-start | bytes 196
  13.0 21.0 %all-to-all-start = ((bf16[4,2,32768]{2,1,0:T(2,128)(2,1)}), bf16[4,2,32768]{2,1,0:T(2,128)(2,1)}, u32[]{:S(2)}, u32[]{:S(2)}) async-start(bf16[4,2,32768]{2,1,0:T(2,128)(2,1)} %reshape.136), calls=%async_computation | async-start | bytes 1048576 | tf_op jit(solution)/shard_map/all_to_all | solution.py:99
  25.8 32.0 %copy-start.6 = (bf16[2,256,256]{2,1,0:T(8,128)(2,1)S(1)}, bf16[2,256,256]{2,1,0:T(8,128)(2,1)}, u32[]{:S(2)}) copy-start(bf16[2,256,256]{2,1,0:T(8,128)(2,1)} %param.18) | copy-start | bytes 786436
  25.8 32.0 %copy-start.7 = (bf16[16,256]{1,0:T(8,128)(2,1)S(1)}, bf16[16,256]{1,0:T(8,128)(2,1)}, u32[]{:S(2)}) copy-start(bf16[16,256]{1,0:T(8,128)(2,1)} %param.17) | copy-start | bytes 24580
  25.8 32.0 %copy-start.9 = (bf16[256]{0:T(256)(128)(2,1)S(1)}, bf16[256]{0:T(256)(128)(2,1)}, u32[]{:S(2)}) copy-start(bf16[256]{0:T(256)(128)(2,1)} %param.19) | copy-start | bytes 1540
  34.0 130.0 %all-to-all-start.2 = ((bf16[128,2,4096]{2,1,0:T(2,128)(2,1)}), bf16[128,2,4096]{2,1,0:T(2,128)(2,1)S(1)}, u32[]{:S(2)}, u32[]{:S(2)}) async-start(bf16[128,2,4096]{2,1,0:T(2,128)(2,1)} %scatter_fusion.1), calls=%async_computation.2 | async-start | bytes 4194304 | tf_op jit(solution)/shard_map/all_to_all | solution.py:127
  57.7 87.1 %copy-start.1 = (bf16[16,4,4096]{2,1,0:T(4,128)(2,1)S(1)}, bf16[16,4,4096]{2,1,0:T(4,128)(2,1)}, u32[]{:S(2)}) copy-start(bf16[16,4,4096]{2,1,0:T(4,128)(2,1)} %param.11) | copy-start | bytes 1572868
  164.0 194.8 %all-to-all-start.1 = ((bf16[128,5,4096]{2,1,0:T(8,128)(2,1)}), bf16[128,5,4096]{2,1,0:T(8,128)(2,1)}, u32[]{:S(2)}, u32[]{:S(2)}) async-start(bf16[128,5,4096]{2,1,0:T(8,128)(2,1)} %scatter_fusion), calls=%async_computation.1 | async-start | bytes 16777216 | tf_op jit(solution)/shard_map/all_to_all | solution.py:126
  415.8 3.4 copy-start
  452.6 5.3 %collective-permute-start = (f32[4,64,1]{2,1,0:T(8,128)S(1)}, f32[4,64,1]{2,1,0:T(8,128)S(1)}, u32[]{:S(2)}, u32[]{:S(2)}) collective-permute-start(f32[4,64,1]{2,1,0:T(8,128)S(1)} %get-tuple-element.78), channel_id=1, source_target_pairs={{1,0},{2,1},{3,2},{4,3},{5,4},{6,5},{7,6},{8,7},{9,8},{10,9},{11,1... | collective-permute-start | bytes 3080 | tf_op jit(solution)/shard_map/ppermute | solution.py:22
  454.5 8.4 %collective-permute-start.1 = (f32[4,64,1]{2,1,0:T(8,128)S(1)}, f32[4,64,1]{2,1,0:T(8,128)S(1)}, u32[]{:S(2)}, u32[]{:S(2)}) collective-permute-start(f32[4,64,1]{2,1,0:T(8,128)S(1)} %get-tuple-element.79), channel_id=1, source_target_pairs={{0,1},{1,2},{2,3},{3,4},{4,5},{5,6},{6,7},{7,8},{8,9},{9,10},{10,1... | collective-permute-start | bytes 3080 | tf_op jit(solution)/shard_map/ppermute | solution.py:19
  463.3 4.4 collective-permute-start.2
  465.2 8.4 %collective-permute-start.3 = (f32[4,64,1]{2,1,0:T(8,128)S(1)}, f32[4,64,1]{2,1,0:T(8,128)S(1)}, u32[]{:S(2)}, u32[]{:S(2)}) collective-permute-start(f32[4,64,1]{2,1,0:T(8,128)S(1)} %get-tuple-element.77), channel_id=1, source_target_pairs={{0,1},{1,2},{2,3},{3,4},{4,5},{5,6},{6,7},{7,8},{8,9},{9,10},{10,1... | collective-permute-start | bytes 3080 | tf_op jit(solution)/shard_map/ppermute | solution.py:19
where the time goes:
time: 477 us; the launch traced here: 475 us
  waiting for transfers between devices  181 us (38%)
  local copies, waits for them, and re-layouts  129 us (27%)
  matrix products  62.6 us (13%)
  other arithmetic  51.6 us (11%)
  starting transfers between devices  36.4 us (8%)
  blocking collectives  12.8 us (3%)
    all_to_all x1, waiting for transfers between devices, per_device(): lax.all_to_all(raw_out, 'tile', split_axis=0, concat_axis=0, tiled=True)  170 us
    reduce_sum x4, other arithmetic, huber_merge(): jnp.sum(huber_w, 0) + prior_weight  30.6 us
    unnamed x26, local copies, waits for them, and re-layouts  26.2 us
    dot_general x16, matrix products, one_scene(): logits = jnp.dot(hidden, w_out, preferred_element_type=jnp.float32)  25.4 us
    dot_general x16, matrix products, one_scene(): jnp.dot(hidden, w_hidden[repeat], preferred_element_type=jnp.float32)  24.6 us
    convert_element_type x1, local copies, waits for them, and re-layouts, reproject(): return jnp.einsum('nij,ncjl->ncil', rows_matrix, half_done, preferred_ele...  18.1 us
    reshape x1, local copies, waits for them, and re-layouts, per_device(): raw_in.reshape(buffer_rows, plane_count, side_cells, side_cells)  15.7 us
    all_gather x1, blocking collectives, per_device(): weights = lax.all_gather(partial_weights, 'band', axis=1, tiled=True)  12.8 us
  transfers between devices with their start and end apart: 7, of which 3 were waited for; matrix products, arithmetic and copies ran while one was open for 29% of the time, Pallas kernels for 0%

commit v1 on v0

--- a/solution.py
+++ b/solution.py
@@ -102,7 +102,21 @@
         valid_rows, lax.axis_index("band") * row_count, row_count, 1
     )
     partial_weights = scene_weights(by_rows, valid_here, recency, w_in, w_hidden, w_out, side_cells)
-    weights = lax.all_gather(partial_weights, "band", axis=1, tiled=True)
+    degree = lax.axis_size("band")
+    so_far_all = [(c, (c + 1) % degree) for c in range(degree)]
+    chunks = [(c, (c - 1) % degree) for c in range(degree)]
+    val, h_now = ([partial_weights], [partial_weights])
+    for _ in range(degree // 2):
+        later = lax.ppermute(val[-1], axis_name="band", perm=so_far_all)
+        val.append(later)
+    q = 0
+    while q < (degree - 1) // 2:
+        w2 = lax.ppermute(h_now[-1], axis_name="band", perm=chunks)
+        h_now.append(w2)
+        q += 1
+    current_block = jnp.concatenate([*val[::-1], *h_now[1:]], axis=1)
+    tmp = lax.axis_index("band")
+    weights = jnp.roll(current_block, shift=(tmp - degree // 2) * partial_weights.shape[1], axis=1)
     plane_count = group_bands + 1
     planes = jnp.concatenate([granules, weights[:, None, :]], 1)
     entry_count = scenes * intersection_count

time: 477 us -> 475 us (level)
  blocking collectives: 12.8 us -> 0 us
  starting transfers between devices: 36.4 us -> 41.8 us
  waiting for transfers between devices: 181 us -> 186 us
    all_gather x1 -> x0, blocking collectives: 12.8 us -> none  [per_device(): weights = lax.all_gather(partial_weights, 'band', axis=1, tiled=True)]
    ppermute x0 -> x3, starting transfers between devices: none -> 5.34 us  [the longest x2 2.91 us: per_device(): later = lax.ppermute(val[-1], axis_name='band', perm=so_far_all)]
    ppermute x0 -> x3, waiting for transfers between devices: none -> 5 us  [the longest x2 4.99 us: per_device(): later = lax.ppermute(val[-1], axis_name='band', perm=so_far_all)]
    unnamed x26 -> x33, local copies, waits for them, and re-layouts: 26.2 us -> 26.2 us
  transfers between devices with their start and end apart: 7 -> 10, of which waited for: 3 -> 5; matrix products, arithmetic and copies ran while one was open for 29% -> 29% of each run, Pallas kernels for 0% -> 0%
where the time goes in v1:
time: 475 us; the launch traced here: 472 us
  waiting for transfers between devices  186 us (39%)
  local copies, waits for them, and re-layouts  129 us (27%)
  matrix products  62.6 us (13%)
  other arithmetic  51.6 us (11%)
  starting transfers between devices  41.8 us (9%)
    all_to_all x1, waiting for transfers between devices, per_device(): lax.all_to_all(raw_out, 'tile', split_axis=0, concat_axis=0, tiled=True)  170 us
    reduce_sum x4, other arithmetic, huber_merge(): jnp.sum(huber_w, 0) + prior_weight  30.6 us
    unnamed x33, local copies, waits for them, and re-layouts  26.2 us
    dot_general x16, matrix products, one_scene(): logits = jnp.dot(hidden, w_out, preferred_element_type=jnp.float32)  25.4 us
    dot_general x16, matrix products, one_scene(): jnp.dot(hidden, w_hidden[repeat], preferred_element_type=jnp.float32)  24.6 us
    convert_element_type x1, local copies, waits for them, and re-layouts, reproject(): return jnp.einsum('nij,ncjl->ncil', rows_matrix, half_done, preferred_ele...  18.1 us
    reshape x1, local copies, waits for them, and re-layouts, per_device(): raw_in.reshape(buffer_rows, plane_count, side_cells, side_cells)  15.7 us
    dot_general x1, matrix products, reproject(): jnp.einsum('nij,ncjl->ncil', rows_matrix, half_done, preferred_element_ty...  12.5 us
  transfers between devices with their start and end apart: 10, of which 5 were waited for; matrix products, arithmetic and copies ran while one was open for 29% of the time, Pallas kernels for 0%

profile of v1, /device:TPU:8, one launch (start us, length us, event | category | flops | bytes accessed | tf_op | source)
XLA Modules:
  0.0 472.2 jit_solution(12859525041134505195)
XLA Ops:
  0.0 6.5 %copy.56 = bf16[16,4,4096]{0,1,2:T(4,128)(2,1)} copy(bf16[16,4,4096]{2,1,0:T(4,128)(2,1)} %param.11) | data formatting | bytes 1048576 | tf_op args[0]
  6.5 6.5 %reshape.136 = bf16[4,2,32768]{2,1,0:T(2,128)(2,1)} reshape(bf16[4096,4,16]{2,1,0:T(4,128)(2,1)} %bitcast.85) | data formatting | bytes 1048576
  13.0 4.3 all-to-all-start
  19.9 2.4 pad_maximum_fusion.1
  22.3 3.4 broadcast_in_dim.40
  25.8 8.2 %scatter_fusion.1 = bf16[128,2,4096]{2,1,0:T(2,128)(2,1)} fusion(bf16[128,2,4096]{2,1,0:T(2,128)(2,1)} %broadcast_in_dim.40, s32[64]{0:T(128)S(1)} %fusion.59, bf16[64,2,4096]{2,1,0:T(2,128)(2,1)S(1)} %pad_maximum_fusion.1), kind=kCustom, calls=%fused_computation.1 | custom fusion | bytes 3145984 | tf_op jit(solution)/shard_map/scatter | solution.py:138
  34.0 12.1 %all-to-all-start.2 = ((bf16[128,2,4096]{2,1,0:T(2,128)(2,1)}), bf16[128,2,4096]{2,1,0:T(2,128)(2,1)S(1)}, u32[]{:S(2)}, u32[]{:S(2)}) async-start(bf16[128,2,4096]{2,1,0:T(2,128)(2,1)} %scatter_fusion.1), calls=%async_computation.2 | async-start | bytes 4194304 | tf_op jit(solution)/shard_map/all_to_all | solution.py:141
  46.1 5.4 %reshape.137 = bf16[4096,4,16]{2,1,0:T(4,128)(2,1)} reshape(bf16[4,2,32768]{2,1,0:T(2,128)(2,1)} %all-to-all-done) | data formatting | bytes 1048576
  51.5 6.1 %copy.57 = bf16[16,4,4,1024]{3,2,1,0:T(4,128)(2,1)S(1)} copy(bf16[16,4,4,1024]{0,2,3,1:T(4,128)(2,1)} %bitcast.84) | data formatting | bytes 1048576 | tf_op jit(solution)/shard_map/all_to_all | solution.py:99
  57.8 74.0 %while.10 = (s32[]{:T(128)}, bf16[16,1024]{1,0:T(8,128)(2,1)S(1)}, bf16[16,16,1024]{2,1,0:T(8,128)(2,1)S(1)}, bf16[16,256]{1,0:T(8,128)(2,1)S(1)}, bf16[2,256,25...) while((s32[]{:T(128)}, bf16[16,1024]{1,0:T(8,128)(2,1)S(1)}, ...), condition=%wide.region_3.4_spmd, body=%wide.region_2.3_spmd.sunk | while | flops 281285632 | bytes 1384577 | solution.py:46
  63.9 1.6 fusion.80
  68.6 1.6 fusion.80
  77.8 1.6 fusion.80
  82.4 1.6 fusion.80
  87.0 1.6 fusion.80
  91.7 1.6 fusion.80
  96.3 1.6 fusion.80
  100.9 1.6 fusion.80
  119.4 1.6 fusion.80
  131.7 2.1 collective-permute-start
  133.8 3.1 collective-permute-done
  137.7 2.4 collective-permute-start.2
  140.2 1.9 collective-permute-done.1
  143.0 2.4 broadcast_in_dim.20.clone
  145.4 4.3 broadcast_in_dim.16
  149.7 11.9 %scatter_fusion = bf16[128,5,4096]{2,1,0:T(8,128)(2,1)} fusion(bf16[128,5,4096]{2,1,0:T(8,128)(2,1)} %broadcast_in_dim.16, s32[64]{0:T(128)S(1)} %fusion.59, bf16[64,5,4096]{2,1,0:T(8,128)(2,1)} %bitcast.83), kind=kCustom, calls=%fused_computation | custom fusion | bytes 7864576 | tf_op jit(solution)/shard_map/scatter | solution.py:136
  161.6 10.5 %all-to-all-start.1 = ((bf16[128,5,4096]{2,1,0:T(8,128)(2,1)}), bf16[128,5,4096]{2,1,0:T(8,128)(2,1)}, u32[]{:S(2)}, u32[]{:S(2)}) async-start(bf16[128,5,4096]{2,1,0:T(8,128)(2,1)} %scatter_fusion), calls=%async_computation.1 | async-start | bytes 16777216 | tf_op jit(solution)/shard_map/all_to_all | solution.py:140
  172.1 4.0 copy.64
  176.2 2.7 fusion.60
  178.8 3.9 copy.74
  182.8 3.8 copy.75
  186.6 169.9 %all-to-all-done.1 = bf16[128,5,4096]{2,1,0:T(8,128)(2,1)} async-done(((bf16[128,5,4096]{2,1,0:T(8,128)(2,1)}), bf16[128,5,4096]{2,1,0:T(8,128)(2,1)}, u32[]{:S(2)}, u32[]{:S(2)}) %all-to-all-start.1) | async-done | bytes 5242912 | tf_op jit(solution)/shard_map/all_to_all | solution.py:140
  356.4 10.6 %copy.61 = bf16[128,5,4096]{0,2,1:T(8,128)(2,1)} copy(bf16[128,5,4096]{2,1,0:T(8,128)(2,1)} %all-to-all-done.1) | data formatting | bytes 10485760 | tf_op jit(solution)/shard_map/all_to_all | solution.py:140
  367.1 15.7 %copy.66 = bf16[128,5,64,64]{3,2,1,0:T(8,128)(2,1)} copy(bf16[128,5,64,64]{0,3,2,1:T(8,128)(2,1)} %bitcast.82) | data formatting | bytes 10485760 | tf_op jit(solution)/shard_map/reshape | solution.py:145
  382.8 12.5 %convert_bitcast_fusion = bf16[128,5,64,64]{2,3,1,0:T(8,128)(2,1)} fusion(bf16[128,5,64,64]{3,2,1,0:T(8,128)(2,1)} %copy.66, bf16[128,1,64,64]{3,2,0,1:T(8,128)(2,1)} %copy.75, bf16[128,1,64,64]{3,2,0,1:T(8,128)(2,1)S(1)} %copy.74), kind=kOutput, calls=%fused_computation.29 | convolution fusion | flops 676331520 | bytes 12582912 | tf_op jit(solution)/shard_map/nij,ncjl->ncil/dot_general | solution.py:53
  395.3 18.1 %copy.69 = bf16[128,5,64,64]{0,3,2,1:T(8,128)(2,1)} copy(bf16[128,5,64,64]{2,3,1,0:T(8,128)(2,1)} %convert_bitcast_fusion) | data formatting | bytes 10485760 | tf_op jit(solution)/shard_map/convert_element_type | solution.py:55
  414.9 1.9 fusion.48
  416.9 2.3 fusion.23
  419.2 7.8 %fusion.47 = (f32[4,4096]{1,0:T(4,128)S(1)}, f32[4,4096]{1,0:T(4,128)S(1)}) fusion(f32[4,4096]{1,0:T(4,128)S(1)} %broadcast_divide_fusion, f32[128,4096]{0,1:T(8,128)S(1)} %get-tuple-element.72, bf16[128,5,4096]{0,2,1:T(8,128)(2,1)S(1)} %bitcast.78), kind=kLoop, calls=%fused_computation.53 | loop fusion | flops 16744448 | bytes 6488064 | tf_op jit(solution)/shard_map/reduce_sum | solution.py:65
  427.0 7.6 %fusion.46 = (f32[4,4096]{1,0:T(4,128)S(1)}, f32[4,4096]{1,0:T(4,128)S(1)}) fusion(f32[4,4096]{1,0:T(4,128)S(1)} %add_divide_fusion.5, f32[128,4096]{0,1:T(8,128)S(1)} %get-tuple-element.72, bf16[128,5,4096]{0,2,1:T(8,128)(2,1)S(1)} %bitcast.79), kind=kLoop, calls=%fused_computation.52 | loop fusion | flops 16744448 | bytes 6488064 | tf_op jit(solution)/shard_map/reduce_sum | solution.py:65
  434.7 7.6 %fusion.45 = (f32[4,4096]{1,0:T(4,128)S(1)}, f32[4,4096]{1,0:T(4,128)S(1)}) fusion(f32[4,4096]{1,0:T(4,128)S(1)} %add_divide_fusion.4, f32[128,4096]{0,1:T(8,128)S(1)} %get-tuple-element.72, bf16[128,5,4096]{0,2,1:T(8,128)(2,1)S(1)} %bitcast.80), kind=kLoop, calls=%fused_computation.51 | loop fusion | flops 16744448 | bytes 6488064 | tf_op jit(solution)/shard_map/reduce_sum | solution.py:65
  442.3 7.6 %fusion.44 = (f32[4,4096]{1,0:T(4,128)S(1)}, f32[4,4096]{1,0:T(4,128)S(1)}) fusion(f32[4,4096]{1,0:T(4,128)S(1)} %add_divide_fusion.3, f32[128,4096]{0,1:T(8,128)S(1)} %get-tuple-element.72, bf16[128,5,4096]{0,2,1:T(8,128)(2,1)S(1)} %bitcast.81), kind=kLoop, calls=%fused_computation.50 | loop fusion | flops 16744448 | bytes 6488064 | tf_op jit(solution)/shard_map/reduce_sum | solution.py:65
  450.2 1.9 collective-permute-start.3
  452.1 3.3 collective-permute-start.4
  455.4 5.1 %collective-permute-done.4 = f32[4,64,1]{2,1,0:T(8,128)S(1)} collective-permute-done((f32[4,64,1]{2,1,0:T(8,128)S(1)}, f32[4,64,1]{2,1,0:T(8,128)S(1)}, u32[]{:S(2)}, u32[]{:S(2)}) %collective-permute-start.4) | collective-permute-done | bytes 1056 | tf_op jit(solution)/shard_map/ppermute | solution.py:19
  460.9 1.9 collective-permute-start.5
  462.8 2.4 collective-permute-start.6
  465.3 5.9 %collective-permute-done.6 = f32[4,64,1]{2,1,0:T(8,128)S(1)} collective-permute-done((f32[4,64,1]{2,1,0:T(8,128)S(1)}, f32[4,64,1]{2,1,0:T(8,128)S(1)}, u32[]{:S(2)}, u32[]{:S(2)}) %collective-permute-start.6) | collective-permute-done | bytes 1056 | tf_op jit(solution)/shard_map/ppermute | solution.py:19
  (191 shorter events, 66.7 us)
Async XLA Ops:
  0.0 17.3 %copy-start.4 = (s32[16,4]{0,1:T(4,128)S(1)}, s32[16,4]{0,1:T(4,128)}, u32[]{:S(2)}) copy-start(s32[16,4]{0,1:T(4,128)} %param.14) | copy-start | bytes 772
  0.0 17.4 %copy-start.5 = (s32[16,64]{1,0:T(8,128)S(1)}, s32[16,64]{1,0:T(8,128)}, u32[]{:S(2)}) copy-start(s32[16,64]{1,0:T(8,128)} %param.12) | copy-start | bytes 12292
  0.0 18.3 %copy-start.2 = (bf16[16,4,4096]{2,1,0:T(4,128)(2,1)S(1)}, bf16[16,4,4096]{2,1,0:T(4,128)(2,1)}, u32[]{:S(2)}) copy-start(bf16[16,4,4096]{2,1,0:T(4,128)(2,1)} %param.15) | copy-start | bytes 1572868
  0.0 19.1 %copy-start.3 = (bf16[16,4,4096]{2,1,0:T(4,128)(2,1)S(1)}, bf16[16,4,4096]{2,1,0:T(4,128)(2,1)}, u32[]{:S(2)}) copy-start(bf16[16,4,4096]{2,1,0:T(4,128)(2,1)} %param.16) | copy-start | bytes 1572868
  6.5 27.5 %copy-start.8 = (s32[16]{0:T(128)S(1)}, s32[16]{0:T(128)}, u32[]{:S(2)}) copy-start(s32[16]{0:T(128)} %param.13) | copy-start | bytes 196
  13.0 21.0 %all-to-all-start = ((bf16[4,2,32768]{2,1,0:T(2,128)(2,1)}), bf16[4,2,32768]{2,1,0:T(2,128)(2,1)}, u32[]{:S(2)}, u32[]{:S(2)}) async-start(bf16[4,2,32768]{2,1,0:T(2,128)(2,1)} %reshape.136), calls=%async_computation | async-start | bytes 1048576 | tf_op jit(solution)/shard_map/all_to_all | solution.py:99
  25.8 32.0 %copy-start.6 = (bf16[2,256,256]{2,1,0:T(8,128)(2,1)S(1)}, bf16[2,256,256]{2,1,0:T(8,128)(2,1)}, u32[]{:S(2)}) copy-start(bf16[2,256,256]{2,1,0:T(8,128)(2,1)} %param.18) | copy-start | bytes 786436
  25.8 32.0 %copy-start.7 = (bf16[16,256]{1,0:T(8,128)(2,1)S(1)}, bf16[16,256]{1,0:T(8,128)(2,1)}, u32[]{:S(2)}) copy-start(bf16[16,256]{1,0:T(8,128)(2,1)} %param.17) | copy-start | bytes 24580
  25.8 32.0 %copy-start.9 = (bf16[256]{0:T(256)(128)(2,1)S(1)}, bf16[256]{0:T(256)(128)(2,1)}, u32[]{:S(2)}) copy-start(bf16[256]{0:T(256)(128)(2,1)} %param.19) | copy-start | bytes 1540
  34.0 127.6 %all-to-all-start.2 = ((bf16[128,2,4096]{2,1,0:T(2,128)(2,1)}), bf16[128,2,4096]{2,1,0:T(2,128)(2,1)S(1)}, u32[]{:S(2)}, u32[]{:S(2)}) async-start(bf16[128,2,4096]{2,1,0:T(2,128)(2,1)} %scatter_fusion.1), calls=%async_computation.2 | async-start | bytes 4194304 | tf_op jit(solution)/shard_map/all_to_all | solution.py:141
  57.7 84.7 %copy-start.1 = (bf16[16,4,4096]{2,1,0:T(4,128)(2,1)S(1)}, bf16[16,4,4096]{2,1,0:T(4,128)(2,1)}, u32[]{:S(2)}) copy-start(bf16[16,4,4096]{2,1,0:T(4,128)(2,1)} %param.11) | copy-start | bytes 1572868
  131.7 5.2 %collective-permute-start = (bf16[16,1024]{1,0:T(8,128)(2,1)S(1)}, bf16[16,1024]{1,0:T(8,128)(2,1)S(1)}, u32[]{:S(2)}, u32[]{:S(2)}) collective-permute-start(bf16[16,1024]{1,0:T(8,128)(2,1)S(1)} %get-tuple-element.47), channel_id=1, source_target_pairs={{0,64},{64,128},{128,192},{192,0},{1,65},{65,129},{129,193},{193,1... | collective-permute-start | bytes 98312 | tf_op jit(solution)/shard_map/ppermute | solution.py:110
  136.9 5.1 %collective-permute-start.1 = (bf16[16,1024]{1,0:T(8,128)(2,1)S(1)}, bf16[16,1024]{1,0:T(8,128)(2,1)S(1)}, u32[]{:S(2)}, u32[]{:S(2)}) collective-permute-start(bf16[16,1024]{1,0:T(8,128)(2,1)S(1)} %collective-permute-done), channel_id=1, source_target_pairs={{0,64},{64,128},{128,192},{192,0},{1,65},{65,129},{129,193},{193,1... | collective-permute-start | bytes 98312 | tf_op jit(solution)/shard_map/ppermute | solution.py:110
  137.7 4.3 collective-permute-start.2
  161.6 194.8 %all-to-all-start.1 = ((bf16[128,5,4096]{2,1,0:T(8,128)(2,1)}), bf16[128,5,4096]{2,1,0:T(8,128)(2,1)}, u32[]{:S(2)}, u32[]{:S(2)}) async-start(bf16[128,5,4096]{2,1,0:T(8,128)(2,1)} %scatter_fusion), calls=%async_computation.1 | async-start | bytes 16777216 | tf_op jit(solution)/shard_map/all_to_all | solution.py:140
  413.4 3.4 copy-start
  450.2 5.3 %collective-permute-start.3 = (f32[4,64,1]{2,1,0:T(8,128)S(1)}, f32[4,64,1]{2,1,0:T(8,128)S(1)}, u32[]{:S(2)}, u32[]{:S(2)}) collective-permute-start(f32[4,64,1]{2,1,0:T(8,128)S(1)} %get-tuple-element.78), channel_id=1, source_target_pairs={{1,0},{2,1},{3,2},{4,3},{5,4},{6,5},{7,6},{8,7},{9,8},{10,9},{11,1... | collective-permute-start | bytes 3080 | tf_op jit(solution)/shard_map/ppermute | solution.py:22
  452.1 8.4 %collective-permute-start.4 = (f32[4,64,1]{2,1,0:T(8,128)S(1)}, f32[4,64,1]{2,1,0:T(8,128)S(1)}, u32[]{:S(2)}, u32[]{:S(2)}) collective-permute-start(f32[4,64,1]{2,1,0:T(8,128)S(1)} %get-tuple-element.79), channel_id=1, source_target_pairs={{0,1},{1,2},{2,3},{3,4},{4,5},{5,6},{6,7},{7,8},{8,9},{9,10},{10,1... | collective-permute-start | bytes 3080 | tf_op jit(solution)/shard_map/ppermute | solution.py:19
  460.9 4.4 collective-permute-start.5
  462.8 8.4 %collective-permute-start.6 = (f32[4,64,1]{2,1,0:T(8,128)S(1)}, f32[4,64,1]{2,1,0:T(8,128)S(1)}, u32[]{:S(2)}, u32[]{:S(2)}) collective-permute-start(f32[4,64,1]{2,1,0:T(8,128)S(1)} %get-tuple-element.77), channel_id=1, source_target_pairs={{0,1},{1,2},{2,3},{3,4},{4,5},{5,6},{6,7},{7,8},{8,9},{9,10},{10,1... | collective-permute-start | bytes 3080 | tf_op jit(solution)/shard_map/ppermute | solution.py:19
